TPU v7x, 256 devices: a whole 4x4x8 slice. The times are simulated.
256 devices in a mesh: docs: 64 (over z, y, core), rep: 4 (over x).
Axes of the slice: x: 4, y: 4, z: 8, core: 2. Of those that a mesh axis runs over, the one named last changes fastest.
Arguments:
- queries: bfloat16 [32768, 1024], P(('docs', 'rep')), may hold values from -6 to 6
- adapter: bfloat16 [1024, 1024], replicated, may hold values from -0.1875 to 0.1875
- doc_table: bfloat16 [65536, 1024], P(('docs', 'rep')), may hold values from -6 to 6
- routes: int32 [32768, 4], P(('docs', 'rep')), may hold values from 0 to 255, all different within a row; in each aligned block of 128 rows (0 to 127, 128 to 255, ...) at most 4 rows name the same one
- doc_rows: int32 [32768, 4, 16], P(('docs', 'rep')), may hold values from 0 to 255, as said below
- labels: int32 [32768, 4, 16], P(('docs', 'rep')), may hold values from 0 to 4
Outputs:
- losses: float32 [32768], P(('docs', 'rep'))
- query_grads: bfloat16 [32768, 1024], P(('docs', 'rep'))
- adapter_grad: bfloat16 [1024, 1024], P('docs')
Inputs may be any that keep to these rules, and one draw needn't show every extreme that they name: `routes`: each query names 4 different owners; among the queries of one device no owner is named more than 4 times, and in every draw some owner is named exactly 4 times by some device's queries. `doc_rows`: the 16 rows of one query at one owner are distinct.
All inputs are finite; a program needn't handle non-finite values.
Results may differ from a plain program's by a relative error of at most 0.024.
Values may be sent and summed in bfloat16 or wider, within the bound.
No kernel may reach another device: no remote copies, remote signals or barrier semaphores. Data moves between devices by JAX's collectives and lax.ppermute only.
A program may use at most 128 MiB of HBM per device.

v0:
```python
import math
import jax
import jax.numpy as jnp
from jax import lax
from jax.sharding import PartitionSpec as P

EPSILON = 1e-06
LOSS_SCALE = 128.0


def unit_rows(rows):
    widened = rows.astype(jnp.float32)
    return (
        widened / jnp.sqrt(jnp.mean(widened * widened, axis=-1, keepdims=True) + EPSILON)
    ).astype(jnp.bfloat16)


def on_device(queries, adapter, doc_table, routes, doc_rows, labels):
    doc_groups = lax.axis_size("docs")
    rep_groups = lax.axis_size("rep")
    devices = doc_groups * rep_groups
    query_rows, feature_width = queries.shape
    fanout = routes.shape[1]
    per_owner = doc_rows.shape[2]
    doc_count = doc_table.shape[0]
    capacity = max(2, 2 * query_rows * fanout // devices)
    slots_all = devices * capacity
    score_scale = 2.0 / math.sqrt(feature_width)
    adapted = jnp.dot(queries, adapter, preferred_element_type=jnp.float32)
    radius = jnp.sqrt(jnp.mean(adapted * adapted, axis=-1, keepdims=True) + EPSILON)
    unit_exact = adapted / radius
    unit_query = unit_exact.astype(jnp.bfloat16)
    owner_hits = (routes[:, :, None] == jnp.arange(devices, dtype=jnp.int32)[None, None, :]).astype(
        jnp.int32
    )
    per_query = jnp.sum(owner_hits, axis=1)
    row_index = jnp.arange(query_rows, dtype=jnp.int32)
    lower_table = (row_index[:, None] > row_index[None, :]).astype(jnp.float32)
    earlier = jnp.dot(
        lower_table, per_query.astype(jnp.float32), precision=lax.Precision.HIGHEST
    ).astype(jnp.int32)
    slot_index = jnp.sum(earlier[:, None, :] * owner_hits, axis=-1)
    placed = routes * capacity + slot_index
    target_slot = placed.reshape(-1)
    repeated = jnp.broadcast_to(
        unit_query[:, None, :], (query_rows, fanout, feature_width)
    ).reshape(-1, feature_width)
    outgoing = jnp.zeros((slots_all, feature_width), jnp.bfloat16).at[target_slot].set(repeated)
    outgoing_ids = (
        jnp.zeros((slots_all, per_owner), jnp.int32)
        .at[target_slot]
        .set(doc_rows.reshape(-1, per_owner))
    )
    outgoing = outgoing.reshape(doc_groups, rep_groups, capacity, feature_width)
    outgoing_ids = outgoing_ids.reshape(doc_groups, rep_groups, capacity, per_owner)
    arrived, arrived_ids = (
        lax.all_to_all(
            lax.all_to_all(outgoing, "docs", split_axis=0, concat_axis=0, tiled=True),
            "rep",
            split_axis=1,
            concat_axis=1,
            tiled=True,
        ),
        lax.all_to_all(
            lax.all_to_all(outgoing_ids, "docs", split_axis=0, concat_axis=0, tiled=True),
            "rep",
            split_axis=1,
            concat_axis=1,
            tiled=True,
        ),
    )
    arrived = arrived.reshape(slots_all, feature_width)
    arrived_ids = arrived_ids.reshape(slots_all, per_owner)
    doc_unit = unit_rows(doc_table)
    block_scores = lax.dot_general(
        arrived, doc_unit, (((1,), (1,)), ((), ())), preferred_element_type=jnp.float32
    )
    scores_out = jnp.take_along_axis(block_scores, arrived_ids, axis=1) * score_scale
    returned = lax.all_to_all(
        lax.all_to_all(
            scores_out.reshape(doc_groups, rep_groups, capacity, per_owner).astype(jnp.bfloat16),
            "docs",
            split_axis=0,
            concat_axis=0,
            tiled=True,
        ),
        "rep",
        split_axis=1,
        concat_axis=1,
        tiled=True,
    ).astype(jnp.float32)
    scores = returned.reshape(slots_all, per_owner)[placed]
    raised = jnp.exp(scores)
    norm_total = jnp.sum(raised, axis=(1, 2))
    label_weight = jnp.exp(labels.astype(jnp.float32))
    target = label_weight / jnp.sum(label_weight, axis=(1, 2), keepdims=True)
    losses = jnp.log(norm_total) - jnp.sum(target * scores, axis=(1, 2))
    weights = (LOSS_SCALE * (raised / norm_total[:, None, None] - target)).astype(jnp.bfloat16)
    weight_slots = (
        jnp.zeros((slots_all, per_owner), jnp.bfloat16)
        .at[target_slot]
        .set(weights.reshape(-1, per_owner))
    )
    weights_in = lax.all_to_all(
        lax.all_to_all(
            weight_slots.reshape(doc_groups, rep_groups, capacity, per_owner),
            "docs",
            split_axis=0,
            concat_axis=0,
            tiled=True,
        ),
        "rep",
        split_axis=1,
        concat_axis=1,
        tiled=True,
    )
    weights_in = weights_in.reshape(slots_all, per_owner)
    spread = (
        jnp.zeros((slots_all, doc_count), jnp.bfloat16)
        .at[jnp.arange(slots_all)[:, None], arrived_ids]
        .set(weights_in)
    )
    pull_out = (jnp.dot(spread, doc_unit, preferred_element_type=jnp.float32) * score_scale).astype(
        jnp.bfloat16
    )
    pull_out = pull_out.reshape(doc_groups, rep_groups, capacity, feature_width)
    pull_back = lax.all_to_all(
        lax.all_to_all(pull_out, "docs", split_axis=0, concat_axis=0, tiled=True),
        "rep",
        split_axis=1,
        concat_axis=1,
        tiled=True,
    )
    pull_rows = pull_back.reshape(slots_all, feature_width)[placed]
    pull_total = jnp.sum(pull_rows.astype(jnp.float32), axis=1)
    projection = jnp.mean(unit_exact * pull_total, axis=-1, keepdims=True)
    adapted_grad = ((pull_total - unit_exact * projection) / radius).astype(jnp.bfloat16)
    query_grads = lax.dot_general(
        adapted_grad, adapter, (((1,), (1,)), ((), ())), preferred_element_type=jnp.float32
    ).astype(jnp.bfloat16)
    inverse_root = 1.0 / math.sqrt(query_rows * devices)
    local_terms = lax.dot_general(
        queries, adapted_grad, (((0,), (0,)), ((), ())), preferred_element_type=jnp.float32
    )
    group_terms = lax.psum(local_terms.astype(jnp.bfloat16), "rep").astype(jnp.float32)
    summed = lax.psum_scatter(group_terms, "docs", scatter_dimension=0, tiled=True)
    adapter_grad = (summed * inverse_root).astype(jnp.bfloat16)
    return (losses, query_grads, adapter_grad)


def solution(mesh):
    placed = (
        P(("docs", "rep"), None),
        P(),
        P(("docs", "rep"), None),
        P(("docs", "rep"), None),
        P(("docs", "rep"), None, None),
        P(("docs", "rep"), None, None),
    )
    return jax.shard_map(
        on_device,
        mesh=mesh,
        in_specs=placed,
        out_specs=(P(("docs", "rep")), P(("docs", "rep"), None), P("docs", None)),
        check_vma=False,
    )
```

profile of v0, /device:TPU:2, one launch (start us, length us, event | category | flops | bytes accessed | tf_op | source)
XLA Modules:
  0.0 777.8 jit_solution(13826968901884588031)
XLA Ops:
  7.2 1.0 convert_reduce_fusion
  8.4 0.9 select_reduce_fusion
  9.3 0.7 compare_select_fusion.3
  10.3 0.9 copy.137
  11.2 1.8 scatter_custom_fusion
  13.0 1.1 reshape.230
  14.1 12.1 %all-to-all-start = ((s32[64,1,256]{2,1,0:T(1,128)}), s32[64,1,256]{2,1,0:T(1,128)S(1)}, u32[]{:S(2)}, u32[]{:S(2)}) async-start(s32[64,1,256]{2,1,0:T(1,128)} %reshape.230), calls=%async_computation | async-start | bytes 131072 | tf_op jit(solution)/shard_map/all_to_all | solution.py:65
  26.2 0.5 multiply_reduce_fusion.1
  26.8 0.8 copy-done.1
  28.0 1.1 reshape.195
  29.1 4.8 scatter_custom_fusion.1
  33.9 4.1 reshape.145
  38.0 10.6 %all-to-all-start.2 = ((bf16[64,4,4,1024]{3,2,1,0:T(4,128)(2,1)}), bf16[64,4,4,1024]{3,2,1,0:T(4,128)(2,1)}, u32[]{:S(2)}, u32[]{:S(2)}) async-start(bf16[64,4,4,1024]{3,2,1,0:T(4,128)(2,1)} %reshape.145), calls=%async_computation.2 | async-start | bytes 4194304 | tf_op jit(solution)/shard_map/all_to_all | solution.py:58
  48.6 0.5 broadcast.163
  49.1 0.8 reduce.4
  50.6 0.8 reshape.232
  51.4 48.4 %all-to-all-done.2 = bf16[64,4,4,1024]{3,2,1,0:T(4,128)(2,1)} async-done(((bf16[64,4,4,1024]{3,2,1,0:T(4,128)(2,1)}), bf16[64,4,4,1024]{3,2,1,0:T(4,128)(2,1)}, u32[]{:S(2)}, u32[]{:S(2)}) %all-to-all-start.2) | async-done | bytes 2097184 | tf_op jit(solution)/shard_map/all_to_all | solution.py:58
  99.8 4.8 all-to-all-start.1
  104.6 3.7 copy.139
  108.3 0.5 all-to-all-done.1
  108.8 5.9 all-to-all-start.3
  114.8 0.7 reshape.163
  115.4 0.6 fusion.12
  116.2 0.8 reduce.5
  117.8 1.0 compare_select_fusion
  119.0 18.1 %all-to-all-done.3 = bf16[64,4,4,1024]{3,2,0,1:T(4,128)(2,1)} async-done(((bf16[64,4,4,1024]{3,2,0,1:T(4,128)(2,1)}), bf16[64,4,4,1024]{3,2,0,1:T(4,128)(2,1)}, u32[]{:S(2)}, u32[]{:S(2)}) %all-to-all-start.3) | async-done | bytes 2097184 | tf_op jit(solution)/shard_map/all_to_all | solution.py:57
  137.1 4.1 copy.140
  141.2 4.0 reshape.146
  145.2 2.5 fusion.15
  147.7 129.5 %gather_fusion.2 = f32[16384]{0:T(1024)S(1)} fusion(f32[1024,256]{1,0:T(8,128)S(1)} %fusion.15, s32[16384]{0:T(1024)S(1)} %reshape.177), kind=kCustom, calls=%fused_computation.2 | custom fusion | bytes 262144 | tf_op jit(solution)/shard_map/jit(take_along_axis)/gather | solution.py:78
  278.2 0.8 reshape.234
  279.0 6.8 all-to-all-start.4
  286.0 9.4 %all-to-all-done.4 = bf16[64,2,128]{2,1,0:T(2,128)(2,1)S(1)} async-done(((bf16[64,2,128]{2,1,0:T(2,128)(2,1)}), bf16[64,2,128]{2,1,0:T(2,128)(2,1)S(1)}, u32[]{:S(2)}, u32[]{:S(2)}) %all-to-all-start.4) | async-done | bytes 32800 | tf_op jit(solution)/shard_map/all_to_all | solution.py:80
  295.8 0.7 reshape.236
  296.6 4.7 all-to-all-start.5
  301.4 3.9 all-to-all-done.5
  305.7 1.0 gather_fusion
  307.1 2.0 scatter_custom_fusion.2
  309.0 0.8 reshape.238
  309.8 4.6 all-to-all-start.6
  314.5 9.4 %all-to-all-done.6 = bf16[64,2,128]{2,1,0:T(2,128)(2,1)S(1)} async-done(((bf16[64,2,128]{2,1,0:T(2,128)(2,1)}), bf16[64,2,128]{2,1,0:T(2,128)(2,1)S(1)}, u32[]{:S(2)}, u32[]{:S(2)}) %all-to-all-start.6) | async-done | bytes 32800 | tf_op jit(solution)/shard_map/all_to_all | solution.py:105
  324.5 0.7 reshape.240
  325.2 4.7 all-to-all-start.7
  330.3 3.6 all-to-all-done.7
  334.4 112.7 %scatter_custom_fusion.3 = bf16[262144]{0:T(1024)(128)(2,1)S(1)} fusion(s32[16384]{0:T(1024)S(1)} %reshape.207, bf16[16384]{0:T(1024)(128)(2,1)S(1)} %reshape.209, bf16[]{:T(256)} %constant.18.clone.1), kind=kCustom, calls=%fused_computation.27 | custom fusion | bytes 524290
  447.1 1.0 reshape.158
  448.1 3.2 multiply_convert_fusion
  451.3 4.1 reshape.153
  455.4 56.1 %all_to_all.50 = bf16[64,4,4,1024]{3,2,1,0:T(4,128)(2,1)S(1)} all-to-all(bf16[64,4,4,1024]{3,2,1,0:T(4,128)(2,1)} %reshape.153), channel_id=1, replica_groups=mesh['docs'=64,'rep'=4] {'docs'}, dimensions={0} | all-to-all | bytes 4194304 | tf_op jit(solution)/shard_map/all_to_all | solution.py:128
  511.5 0.8 copy.155
  512.3 27.9 %all_to_all.51 = bf16[64,4,4,1024]{3,2,0,1:T(4,128)(2,1)S(1)} all-to-all(bf16[64,4,4,1024]{3,2,0,1:T(4,128)(2,1)S(1)} %copy.155), channel_id=1, replica_groups=mesh['docs'=64,'rep'=4] {'rep'}, dimensions={1} | all-to-all | bytes 4194304 | tf_op jit(solution)/shard_map/all_to_all | solution.py:127
  540.2 2.5 copy.156
  542.7 4.0 reshape.154
  546.7 5.3 gather_fusion.1
  552.0 2.7 reshape.219
  554.8 2.9 reduce_sum.88
  558.0 2.2 convert_bitcast_fusion
  560.2 59.0 %all-reduce.2.cloned.1.call-done = bf16[1024,1024]{0,1:T(8,128)(2,1)} async-done(((bf16[1024,1024]{0,1:T(8,128)(2,1)}), bf16[1024,1024]{0,1:T(8,128)(2,1)}) %all-reduce.2.cloned.1.call-update) | async-done | bytes 2097168 | tf_op jit(solution)/shard_map/psum | solution.py:145
  619.3 4.1 copy.158
  623.4 0.5 log_subtract_fusion
  623.9 1.5 convolution_convert_fusion
  625.5 143.6 %reduce-scatter.4.cloned.1.call-done = f32[16,1024]{1,0:T(8,128)} async-done(((f32[1024,1024]{1,0:T(8,128)}), f32[16,1024]{1,0:T(8,128)}) %reduce-scatter.4.cloned.1.call-update) | async-done | bytes 65552
  769.1 1.0 copy.159
  770.2 0.7 copy.157
  (89 shorter events, 7.2 us)
Async XLA Ops:
  7.2 19.0 %copy-start = (bf16[1024,1024]{1,0:T(8,128)(2,1)S(1)}, bf16[1024,1024]{1,0:T(8,128)(2,1)}, u32[]{:S(2)}) copy-start(bf16[1024,1024]{1,0:T(8,128)(2,1)} %param.7) | copy-start | bytes 6291460
  7.2 19.0 %copy-start.10 = (bf16[128,1024]{1,0:T(8,128)(2,1)S(1)}, bf16[128,1024]{1,0:T(8,128)(2,1)}, u32[]{:S(2)}) copy-start(bf16[128,1024]{1,0:T(8,128)(2,1)} %param.6) | copy-start | bytes 786436
  10.3 18.8 %copy-start.16 = (s32[512,1]{0,1:T(1,128)}, s32[512,1]{0,1:T(1,128)S(1)}, u32[]{:S(2)}) copy-start(s32[512,1]{0,1:T(1,128)S(1)} %compare_select_fusion.2) | copy-start | bytes 6148
  14.1 24.0 %all-to-all-start = ((s32[64,1,256]{2,1,0:T(1,128)}), s32[64,1,256]{2,1,0:T(1,128)S(1)}, u32[]{:S(2)}, u32[]{:S(2)}) async-start(s32[64,1,256]{2,1,0:T(1,128)} %reshape.230), calls=%async_computation | async-start | bytes 131072 | tf_op jit(solution)/shard_map/all_to_all | solution.py:65
  26.7 0.8 copy-start.1
  26.8 0.8 copy-start.14
  38.0 61.7 %all-to-all-start.2 = ((bf16[64,4,4,1024]{3,2,1,0:T(4,128)(2,1)}), bf16[64,4,4,1024]{3,2,1,0:T(4,128)(2,1)}, u32[]{:S(2)}, u32[]{:S(2)}) async-start(bf16[64,4,4,1024]{3,2,1,0:T(4,128)(2,1)} %reshape.145), calls=%async_computation.2 | async-start | bytes 4194304 | tf_op jit(solution)/shard_map/all_to_all | solution.py:58
  99.8 9.0 %all-to-all-start.1 = ((s32[4,1,4096]{2,1,0:T(1,128)}), s32[4,1,4096]{2,1,0:T(1,128)S(1)}, u32[]{:S(2)}, u32[]{:S(2)}) async-start(s32[4,1,4096]{2,1,0:T(1,128)} %reshape.232), calls=%async_computation.1 | async-start | bytes 131072 | tf_op jit(solution)/shard_map/all_to_all | solution.py:64
  108.3 7.1 copy-start.8
  108.3 7.7 copy-start.6
  108.8 28.3 %all-to-all-start.3 = ((bf16[64,4,4,1024]{3,2,0,1:T(4,128)(2,1)}), bf16[64,4,4,1024]{3,2,0,1:T(4,128)(2,1)}, u32[]{:S(2)}, u32[]{:S(2)}) async-start(bf16[64,4,4,1024]{3,2,0,1:T(4,128)(2,1)} %copy.139), calls=%async_computation.3 | async-start | bytes 4194304 | tf_op jit(solution)/shard_map/all_to_all | solution.py:57
  116.2 28.9 %copy-start.17 = (f32[256]{0:T(256)}, f32[256]{0:T(256)S(1)}, u32[]{:S(2)}) copy-start(f32[256]{0:T(256)S(1)} %add_sqrt_fusion) | copy-start | bytes 3076
  117.2 0.7 copy-start.4
  147.7 130.2 %copy-start.5 = (s32[4,4,16,64]{3,2,1,0:T(8,128)S(1)}, s32[4,4,16,64]{3,2,1,0:T(8,128)}, u32[]{:S(2)}) copy-start(s32[4,4,16,64]{3,2,1,0:T(8,128)} %copy-done.4) | copy-start | bytes 196612
  277.2 8.6 %copy-start.12 = (s32[512]{0:T(512)S(1)}, s32[512]{0:T(512)}, u32[]{:S(2)}) copy-start(s32[512]{0:T(512)} %reshape.163) | copy-start | bytes 6148
  277.2 8.6 %copy-start.3 = (s32[1024,16,1]{1,0,2:T(8,128)S(1)}, s32[1024,16,1]{1,0,2:T(8,128)}, u32[]{:S(2)}) copy-start(s32[1024,16,1]{1,0,2:T(8,128)} %get-tuple-element.31) | copy-start | bytes 196612
  277.2 24.1 %copy-start.20 = (s32[2]{0:T(128)S(1)}, s32[2]{0:T(128)}, u32[]{:S(2)}) copy-start(s32[2]{0:T(128)} %constant.59) | copy-start | bytes 28
  279.0 16.3 %all-to-all-start.4 = ((bf16[64,2,128]{2,1,0:T(2,128)(2,1)}), bf16[64,2,128]{2,1,0:T(2,128)(2,1)S(1)}, u32[]{:S(2)}, u32[]{:S(2)}) async-start(bf16[64,2,128]{2,1,0:T(2,128)(2,1)} %reshape.234), calls=%async_computation.4 | async-start | bytes 65536 | tf_op jit(solution)/shard_map/all_to_all | solution.py:80
  295.5 11.3 %copy-start.9 = (s32[128,4,16]{0,2,1:T(8,128)S(1)}, s32[128,4,16]{0,2,1:T(8,128)}, u32[]{:S(2)}) copy-start(s32[128,4,16]{0,2,1:T(8,128)} %param.11) | copy-start | bytes 98308
  295.5 11.3 %copy-start.13 = (f32[128]{0:T(128)S(1)}, f32[128]{0:T(128)}, u32[]{:S(2)}) copy-start(f32[128]{0:T(128)} %fusion.12) | copy-start | bytes 1540
  296.6 8.7 %all-to-all-start.5 = ((bf16[4,2,2048]{2,1,0:T(2,128)(2,1)}), bf16[4,2,2048]{2,1,0:T(2,128)(2,1)S(1)}, u32[]{:S(2)}, u32[]{:S(2)}) async-start(bf16[4,2,2048]{2,1,0:T(2,128)(2,1)} %reshape.236), calls=%async_computation.5 | async-start | bytes 65536 | tf_op jit(solution)/shard_map/all_to_all | solution.py:79
  305.4 9.1 %copy-start.19 = (s32[2]{0:T(128)S(1)}, s32[2]{0:T(128)}, u32[]{:S(2)}) copy-start(s32[2]{0:T(128)} %constant.56) | copy-start | bytes 28
  309.8 14.1 %all-to-all-start.6 = ((bf16[64,2,128]{2,1,0:T(2,128)(2,1)}), bf16[64,2,128]{2,1,0:T(2,128)(2,1)S(1)}, u32[]{:S(2)}, u32[]{:S(2)}) async-start(bf16[64,2,128]{2,1,0:T(2,128)(2,1)} %reshape.238), calls=%async_computation.6 | async-start | bytes 65536 | tf_op jit(solution)/shard_map/all_to_all | solution.py:105
  324.2 123.9 %copy-start.7 = (bf16[256,1024]{1,0:T(8,128)(2,1)S(1)}, bf16[256,1024]{1,0:T(8,128)(2,1)}, u32[]{:S(2)}) copy-start(bf16[256,1024]{1,0:T(8,128)(2,1)} %param.8) | copy-start | bytes 1572868
  324.2 123.9 %copy-start.18 = (f32[256]{0:T(256)S(1)}, f32[256]{0:T(256)}, u32[]{:S(2)}) copy-start(f32[256]{0:T(256)} %copy-done.17) | copy-start | bytes 3076
  325.2 8.7 %all-to-all-start.7 = ((bf16[4,2,2048]{2,1,0:T(2,128)(2,1)}), bf16[4,2,2048]{2,1,0:T(2,128)(2,1)S(1)}, u32[]{:S(2)}, u32[]{:S(2)}) async-start(bf16[4,2,2048]{2,1,0:T(2,128)(2,1)} %reshape.240), calls=%async_computation.7 | async-start | bytes 65536 | tf_op jit(solution)/shard_map/all_to_all | solution.py:104
  329.9 289.4 %all-reduce.2.cloned.1.call-start = ((), (), s32[]{:S(2)}) async-start(), calls=%async_computation.11 | async-start | bytes 4194304 | tf_op jit(solution)/shard_map/psum | solution.py:145
  554.8 2.9 copy-start.2
  554.8 2.9 copy-start.15
  554.8 3.2 copy-start.11
  560.2 208.9 %reduce-scatter.4.cloned.1.call-start = ((), (), s32[]{:S(2)}) async-start(), calls=%async_computation.12 | async-start | bytes 4259840
Sparse Core Ops, SparseCore 0:
  560.3 58.9 all-reduce.1
  623.5 145.5 reduce-scatter.3
where the time goes:
time: 779 us; the launch traced here: 778 us
  local copies, waits for them, and re-layouts  309 us (40%)
  waiting for transfers between devices  296 us (38%)
  blocking collectives  83.9 us (11%)
  starting transfers between devices  54.1 us (7%)
  between operations  14.5 us (2%)
  matrix products  10.2 us (1%)
  other arithmetic  10.1 us (1%)
    unnamed x3, waiting for transfers between devices  144 us
    gather x5, local copies, waits for them, and re-layouts, on_device(): jnp.take_along_axis(block_scores, arrived_ids, axis=1) * score_scale  130 us
    unnamed x61, local copies, waits for them, and re-layouts  127 us
    psum x1, waiting for transfers between devices, on_device(): lax.psum(local_terms.astype(jnp.bfloat16), 'rep').astype(jnp.float32)  59 us
    all_to_all x1, blocking collectives, on_device(): lax.all_to_all(pull_out, 'docs', split_axis=0, concat_axis=0, tiled=True)  56.1 us
    all_to_all x1, waiting for transfers between devices, on_device(): lax.all_to_all(outgoing, 'docs', split_axis=0, concat_axis=0, tiled=True)  48.4 us
    all_to_all x1, blocking collectives, on_device(): lax.all_to_all(lax.all_to_all(pull_out, 'docs', split_axis=0, concat_axis...  27.9 us
    all_to_all x1, waiting for transfers between devices, on_device(): lax.all_to_all(lax.all_to_all(outgoing, 'docs', split_axis=0, concat_axis...  18.1 us
  transfers between devices with their start and end apart: 10, of which 9 were waited for; matrix products, arithmetic and copies ran while one was open for 3% of the time, Pallas kernels for 0%

commit v1 on v0

--- a/solution.py
+++ b/solution.py
@@ -142,7 +142,9 @@
     local_terms = lax.dot_general(
         queries, adapted_grad, (((0,), (0,)), ((), ())), preferred_element_type=jnp.float32
     )
-    group_terms = lax.psum(local_terms.astype(jnp.bfloat16), "rep").astype(jnp.float32)
+    group_terms = jnp.sum(lax.all_gather(local_terms.astype(jnp.bfloat16), "rep"), axis=0).astype(
+        jnp.float32
+    )
     summed = lax.psum_scatter(group_terms, "docs", scatter_dimension=0, tiled=True)
     adapter_grad = (summed * inverse_root).astype(jnp.bfloat16)
     return (losses, query_grads, adapter_grad)

time: 779 us -> 839 us (1.077); the launches traced: 778 us -> 829 us
  waiting for transfers between devices: 296 us -> 319 us
  local copies, waits for them, and re-layouts: 309 us -> 323 us
  other arithmetic: 10.1 us -> 23 us
    all_gather x0 -> x1, waiting for transfers between devices: none -> 82.1 us  [on_device(): lax.all_gather(local_terms.astype(jnp.bfloat16), 'rep')]
    psum x1 -> x0, waiting for transfers between devices: 59 us -> none  [on_device(): lax.psum(local_terms.astype(jnp.bfloat16), 'rep').astype(jnp.float32)]
    all_gather x0 -> x1, local copies, waits for them, and re-layouts: none -> 14.6 us  [on_device(): lax.all_gather(local_terms.astype(jnp.bfloat16), 'rep')]
    reduce_sum x0 -> x1, other arithmetic: none -> 12.9 us  [on_device(): jnp.sum(lax.all_gather(local_terms.astype(jnp.bfloat16), 'rep'), axis=0)]
where the time goes in v1:
time: 839 us; the launch traced here: 829 us
  local copies, waits for them, and re-layouts  323 us (38%)
  waiting for transfers between devices  319 us (38%)
  blocking collectives  84.1 us (10%)
  starting transfers between devices  54.8 us (7%)
  other arithmetic  23 us (3%)
  between operations  14.8 us (2%)
  matrix products  10.2 us (1%)
    unnamed x3, waiting for transfers between devices  144 us
    gather x5, local copies, waits for them, and re-layouts, on_device(): jnp.take_along_axis(block_scores, arrived_ids, axis=1) * score_scale  130 us
    unnamed x61, local copies, waits for them, and re-layouts  127 us
    all_gather x1, waiting for transfers between devices, on_device(): lax.all_gather(local_terms.astype(jnp.bfloat16), 'rep')  82.1 us
    all_to_all x1, blocking collectives, on_device(): lax.all_to_all(pull_out, 'docs', split_axis=0, concat_axis=0, tiled=True)  56.1 us
    all_to_all x1, waiting for transfers between devices, on_device(): lax.all_to_all(outgoing, 'docs', split_axis=0, concat_axis=0, tiled=True)  48.4 us
    all_to_all x1, blocking collectives, on_device(): lax.all_to_all(lax.all_to_all(pull_out, 'docs', split_axis=0, concat_axis...  28.1 us
    all_to_all x1, waiting for transfers between devices, on_device(): lax.all_to_all(lax.all_to_all(outgoing, 'docs', split_axis=0, concat_axis...  18.1 us
  transfers between devices with their start and end apart: 10, of which 9 were waited for; matrix products, arithmetic and copies ran while one was open for 3% of the time, Pallas kernels for 0%

profile of v1, /device:TPU:2, one launch (start us, length us, event | category | flops | bytes accessed | tf_op | source)
XLA Modules:
  0.0 829.1 jit_solution(5042912573866345504)
XLA Ops:
  7.2 1.0 convert_reduce_fusion
  8.4 0.9 select_reduce_fusion
  9.3 0.7 compare_select_fusion.3
  10.3 0.9 copy.135
  11.2 1.8 scatter_custom_fusion
  13.0 1.1 reshape.231
  14.1 12.1 %all-to-all-start = ((s32[64,1,256]{2,1,0:T(1,128)}), s32[64,1,256]{2,1,0:T(1,128)S(1)}, u32[]{:S(2)}, u32[]{:S(2)}) async-start(s32[64,1,256]{2,1,0:T(1,128)} %reshape.231), calls=%async_computation | async-start | bytes 131072 | tf_op jit(solution)/shard_map/all_to_all | solution.py:65
  26.2 0.5 multiply_reduce_fusion.1
  26.8 0.8 copy-done.1
  28.0 1.1 reshape.195
  29.1 4.8 scatter_custom_fusion.1
  33.9 4.1 reshape.145
  38.0 10.6 %all-to-all-start.2 = ((bf16[64,4,4,1024]{3,2,1,0:T(4,128)(2,1)}), bf16[64,4,4,1024]{3,2,1,0:T(4,128)(2,1)}, u32[]{:S(2)}, u32[]{:S(2)}) async-start(bf16[64,4,4,1024]{3,2,1,0:T(4,128)(2,1)} %reshape.145), calls=%async_computation.2 | async-start | bytes 4194304 | tf_op jit(solution)/shard_map/all_to_all | solution.py:58
  49.1 0.8 reduce.5
  50.6 0.8 reshape.233
  51.4 48.4 %all-to-all-done.2 = bf16[64,4,4,1024]{3,2,1,0:T(4,128)(2,1)} async-done(((bf16[64,4,4,1024]{3,2,1,0:T(4,128)(2,1)}), bf16[64,4,4,1024]{3,2,1,0:T(4,128)(2,1)}, u32[]{:S(2)}, u32[]{:S(2)}) %all-to-all-start.2) | async-done | bytes 2097184 | tf_op jit(solution)/shard_map/all_to_all | solution.py:58
  99.8 4.8 all-to-all-start.1
  104.6 3.7 copy.137
  108.8 6.3 all-to-all-start.3
  115.2 0.7 reshape.163
  115.9 0.6 fusion.12
  116.7 0.8 reduce.6
  118.3 1.0 compare_select_fusion
  119.5 18.1 %all-to-all-done.3 = bf16[64,4,4,1024]{3,2,0,1:T(4,128)(2,1)} async-done(((bf16[64,4,4,1024]{3,2,0,1:T(4,128)(2,1)}), bf16[64,4,4,1024]{3,2,0,1:T(4,128)(2,1)}, u32[]{:S(2)}, u32[]{:S(2)}) %all-to-all-start.3) | async-done | bytes 2097184 | tf_op jit(solution)/shard_map/all_to_all | solution.py:57
  137.5 4.1 copy.138
  141.6 4.0 reshape.146
  145.6 2.5 fusion.15
  148.1 129.5 %gather_fusion.2 = f32[16384]{0:T(1024)S(1)} fusion(f32[1024,256]{1,0:T(8,128)S(1)} %fusion.15, s32[16384]{0:T(1024)S(1)} %reshape.177), kind=kCustom, calls=%fused_computation.2 | custom fusion | bytes 262144 | tf_op jit(solution)/shard_map/jit(take_along_axis)/gather | solution.py:78
  278.7 0.8 reshape.235
  279.5 6.8 all-to-all-start.4
  286.4 9.4 %all-to-all-done.4 = bf16[64,2,128]{2,1,0:T(2,128)(2,1)S(1)} async-done(((bf16[64,2,128]{2,1,0:T(2,128)(2,1)}), bf16[64,2,128]{2,1,0:T(2,128)(2,1)S(1)}, u32[]{:S(2)}, u32[]{:S(2)}) %all-to-all-start.4) | async-done | bytes 32800 | tf_op jit(solution)/shard_map/all_to_all | solution.py:80
  296.3 0.7 reshape.237
  297.0 4.7 all-to-all-start.5
  301.8 3.9 all-to-all-done.5
  306.1 1.0 gather_fusion
  307.5 2.0 scatter_custom_fusion.2
  309.5 0.8 reshape.239
  310.3 4.6 all-to-all-start.6
  315.0 9.4 %all-to-all-done.6 = bf16[64,2,128]{2,1,0:T(2,128)(2,1)S(1)} async-done(((bf16[64,2,128]{2,1,0:T(2,128)(2,1)}), bf16[64,2,128]{2,1,0:T(2,128)(2,1)S(1)}, u32[]{:S(2)}, u32[]{:S(2)}) %all-to-all-start.6) | async-done | bytes 32800 | tf_op jit(solution)/shard_map/all_to_all | solution.py:105
  324.9 0.7 reshape.241
  325.6 4.7 all-to-all-start.7
  330.9 3.4 all-to-all-done.7
  334.9 112.7 %scatter_custom_fusion.3 = bf16[262144]{0:T(1024)(128)(2,1)S(1)} fusion(s32[16384]{0:T(1024)S(1)} %reshape.207, bf16[16384]{0:T(1024)(128)(2,1)S(1)} %reshape.209, bf16[]{:T(256)} %constant.18.clone.1), kind=kCustom, calls=%fused_computation.27 | custom fusion | bytes 524290
  447.6 1.0 reshape.158
  448.6 3.2 multiply_convert_fusion
  451.8 4.1 reshape.153
  455.9 56.1 %all_to_all.50 = bf16[64,4,4,1024]{3,2,1,0:T(4,128)(2,1)S(1)} all-to-all(bf16[64,4,4,1024]{3,2,1,0:T(4,128)(2,1)} %reshape.153), channel_id=1, replica_groups=mesh['docs'=64,'rep'=4] {'docs'}, dimensions={0} | all-to-all | bytes 4194304 | tf_op jit(solution)/shard_map/all_to_all | solution.py:128
  512.0 0.8 copy.153
  512.8 28.1 %all_to_all.51 = bf16[64,4,4,1024]{3,2,0,1:T(4,128)(2,1)S(1)} all-to-all(bf16[64,4,4,1024]{3,2,0,1:T(4,128)(2,1)S(1)} %copy.153), channel_id=1, replica_groups=mesh['docs'=64,'rep'=4] {'rep'}, dimensions={1} | all-to-all | bytes 4194304 | tf_op jit(solution)/shard_map/all_to_all | solution.py:127
  540.8 2.5 copy.154
  543.4 4.0 reshape.154
  547.3 5.3 gather_fusion.1
  552.7 2.7 reshape.220
  555.4 2.9 reduce_sum.100
  558.6 2.2 convert_bitcast_fusion
  560.9 82.1 %all-gather.3.cloned.1.call-done = bf16[4096,1024]{0,1:T(8,128)(2,1)} async-done(((bf16[1024,1024]{0,1:T(8,128)(2,1)}), bf16[4096,1024]{0,1:T(8,128)(2,1)}) %all-gather.3.cloned.1.call-update) | async-done | bytes 8388624 | tf_op jit(solution)/shard_map/all_gather | solution.py:145
  643.0 14.6 %reshape.213 = bf16[4,1024,1024]{1,0,2:T(4,128)(2,1)} reshape(bf16[4096,1024]{0,1:T(8,128)(2,1)} %all-gather.3.cloned.1.call-done) | data formatting | bytes 16777216 | tf_op jit(solution)/shard_map/all_gather | solution.py:145
  657.5 12.9 %reduce_sum.102 = bf16[1024,1024]{0,1:T(8,128)(2,1)} reduce(bf16[4,1024,1024]{1,0,2:T(4,128)(2,1)} %reshape.213, bf16[]{:T(256)} %constant.18.clone.1), dimensions={0}, to_apply=%region_13.14 | reduce | flops 3145728 | bytes 10485762 | tf_op jit(solution)/shard_map/reduce_sum | solution.py:145
  670.4 4.1 copy.156
  674.5 0.5 log_subtract_fusion
  675.1 1.5 convolution_convert_fusion
  676.6 143.6 %reduce-scatter.4.cloned.1.call-done = f32[16,1024]{1,0:T(8,128)} async-done(((f32[1024,1024]{1,0:T(8,128)}), f32[16,1024]{1,0:T(8,128)}) %reduce-scatter.4.cloned.1.call-update) | async-done | bytes 65552
  820.2 1.0 copy.157
  821.3 0.7 copy.155
  (91 shorter events, 8.3 us)
Async XLA Ops:
  7.2 19.0 %copy-start = (bf16[1024,1024]{1,0:T(8,128)(2,1)S(1)}, bf16[1024,1024]{1,0:T(8,128)(2,1)}, u32[]{:S(2)}) copy-start(bf16[1024,1024]{1,0:T(8,128)(2,1)} %param.7) | copy-start | bytes 6291460
  7.2 19.0 %copy-start.10 = (bf16[128,1024]{1,0:T(8,128)(2,1)S(1)}, bf16[128,1024]{1,0:T(8,128)(2,1)}, u32[]{:S(2)}) copy-start(bf16[128,1024]{1,0:T(8,128)(2,1)} %param.6) | copy-start | bytes 786436
  10.3 18.8 %copy-start.16 = (s32[512,1]{0,1:T(1,128)}, s32[512,1]{0,1:T(1,128)S(1)}, u32[]{:S(2)}) copy-start(s32[512,1]{0,1:T(1,128)S(1)} %compare_select_fusion.2) | copy-start | bytes 6148
  14.1 24.0 %all-to-all-start = ((s32[64,1,256]{2,1,0:T(1,128)}), s32[64,1,256]{2,1,0:T(1,128)S(1)}, u32[]{:S(2)}, u32[]{:S(2)}) async-start(s32[64,1,256]{2,1,0:T(1,128)} %reshape.231), calls=%async_computation | async-start | bytes 131072 | tf_op jit(solution)/shard_map/all_to_all | solution.py:65
  26.7 0.8 copy-start.1
  26.8 0.8 copy-start.14
  38.0 61.7 %all-to-all-start.2 = ((bf16[64,4,4,1024]{3,2,1,0:T(4,128)(2,1)}), bf16[64,4,4,1024]{3,2,1,0:T(4,128)(2,1)}, u32[]{:S(2)}, u32[]{:S(2)}) async-start(bf16[64,4,4,1024]{3,2,1,0:T(4,128)(2,1)} %reshape.145), calls=%async_computation.2 | async-start | bytes 4194304 | tf_op jit(solution)/shard_map/all_to_all | solution.py:58
  99.8 9.0 %all-to-all-start.1 = ((s32[4,1,4096]{2,1,0:T(1,128)}), s32[4,1,4096]{2,1,0:T(1,128)S(1)}, u32[]{:S(2)}, u32[]{:S(2)}) async-start(s32[4,1,4096]{2,1,0:T(1,128)} %reshape.233), calls=%async_computation.1 | async-start | bytes 131072 | tf_op jit(solution)/shard_map/all_to_all | solution.py:64
  108.3 7.6 copy-start.8
  108.3 8.2 copy-start.6
  108.8 28.7 %all-to-all-start.3 = ((bf16[64,4,4,1024]{3,2,0,1:T(4,128)(2,1)}), bf16[64,4,4,1024]{3,2,0,1:T(4,128)(2,1)}, u32[]{:S(2)}, u32[]{:S(2)}) async-start(bf16[64,4,4,1024]{3,2,0,1:T(4,128)(2,1)} %copy.137), calls=%async_computation.3 | async-start | bytes 4194304 | tf_op jit(solution)/shard_map/all_to_all | solution.py:57
  116.7 28.9 %copy-start.17 = (f32[256]{0:T(256)}, f32[256]{0:T(256)S(1)}, u32[]{:S(2)}) copy-start(f32[256]{0:T(256)S(1)} %add_sqrt_fusion) | copy-start | bytes 3076
  117.6 0.7 copy-start.4
  148.1 130.2 %copy-start.5 = (s32[4,4,16,64]{3,2,1,0:T(8,128)S(1)}, s32[4,4,16,64]{3,2,1,0:T(8,128)}, u32[]{:S(2)}) copy-start(s32[4,4,16,64]{3,2,1,0:T(8,128)} %copy-done.4) | copy-start | bytes 196612
  277.6 8.6 %copy-start.12 = (s32[512]{0:T(512)S(1)}, s32[512]{0:T(512)}, u32[]{:S(2)}) copy-start(s32[512]{0:T(512)} %reshape.163) | copy-start | bytes 6148
  277.6 8.6 %copy-start.3 = (s32[1024,16,1]{1,0,2:T(8,128)S(1)}, s32[1024,16,1]{1,0,2:T(8,128)}, u32[]{:S(2)}) copy-start(s32[1024,16,1]{1,0,2:T(8,128)} %get-tuple-element.25) | copy-start | bytes 196612
  277.6 24.1 %copy-start.20 = (s32[2]{0:T(128)S(1)}, s32[2]{0:T(128)}, u32[]{:S(2)}) copy-start(s32[2]{0:T(128)} %constant.60) | copy-start | bytes 28
  279.5 16.3 %all-to-all-start.4 = ((bf16[64,2,128]{2,1,0:T(2,128)(2,1)}), bf16[64,2,128]{2,1,0:T(2,128)(2,1)S(1)}, u32[]{:S(2)}, u32[]{:S(2)}) async-start(bf16[64,2,128]{2,1,0:T(2,128)(2,1)} %reshape.235), calls=%async_computation.4 | async-start | bytes 65536 | tf_op jit(solution)/shard_map/all_to_all | solution.py:80
  296.0 11.3 %copy-start.9 = (s32[128,4,16]{0,2,1:T(8,128)S(1)}, s32[128,4,16]{0,2,1:T(8,128)}, u32[]{:S(2)}) copy-start(s32[128,4,16]{0,2,1:T(8,128)} %param.11) | copy-start | bytes 98308
  296.0 11.3 %copy-start.13 = (f32[128]{0:T(128)S(1)}, f32[128]{0:T(128)}, u32[]{:S(2)}) copy-start(f32[128]{0:T(128)} %fusion.12) | copy-start | bytes 1540
  297.0 8.7 %all-to-all-start.5 = ((bf16[4,2,2048]{2,1,0:T(2,128)(2,1)}), bf16[4,2,2048]{2,1,0:T(2,128)(2,1)S(1)}, u32[]{:S(2)}, u32[]{:S(2)}) async-start(bf16[4,2,2048]{2,1,0:T(2,128)(2,1)} %reshape.237), calls=%async_computation.5 | async-start | bytes 65536 | tf_op jit(solution)/shard_map/all_to_all | solution.py:79
  305.8 9.1 %copy-start.19 = (s32[2]{0:T(128)S(1)}, s32[2]{0:T(128)}, u32[]{:S(2)}) copy-start(s32[2]{0:T(128)} %constant.57) | copy-start | bytes 28
  310.3 14.1 %all-to-all-start.6 = ((bf16[64,2,128]{2,1,0:T(2,128)(2,1)}), bf16[64,2,128]{2,1,0:T(2,128)(2,1)S(1)}, u32[]{:S(2)}, u32[]{:S(2)}) async-start(bf16[64,2,128]{2,1,0:T(2,128)(2,1)} %reshape.239), calls=%async_computation.6 | async-start | bytes 65536 | tf_op jit(solution)/shard_map/all_to_all | solution.py:105
  324.6 123.9 %copy-start.7 = (bf16[256,1024]{1,0:T(8,128)(2,1)S(1)}, bf16[256,1024]{1,0:T(8,128)(2,1)}, u32[]{:S(2)}) copy-start(bf16[256,1024]{1,0:T(8,128)(2,1)} %param.8) | copy-start | bytes 1572868
  324.6 123.9 %copy-start.18 = (f32[256]{0:T(256)S(1)}, f32[256]{0:T(256)}, u32[]{:S(2)}) copy-start(f32[256]{0:T(256)} %copy-done.17) | copy-start | bytes 3076
  325.6 8.7 %all-to-all-start.7 = ((bf16[4,2,2048]{2,1,0:T(2,128)(2,1)}), bf16[4,2,2048]{2,1,0:T(2,128)(2,1)S(1)}, u32[]{:S(2)}, u32[]{:S(2)}) async-start(bf16[4,2,2048]{2,1,0:T(2,128)(2,1)} %reshape.241), calls=%async_computation.7 | async-start | bytes 65536 | tf_op jit(solution)/shard_map/all_to_all | solution.py:104
  330.3 312.6 %all-gather.3.cloned.1.call-start = ((), (), s32[]{:S(2)}) async-start(), calls=%async_computation.11 | async-start | bytes 10485760 | tf_op jit(solution)/shard_map/all_gather | solution.py:145
  555.4 2.9 copy-start.2
  555.4 2.9 copy-start.15
  555.4 3.2 copy-start.11
  560.9 259.4 %reduce-scatter.4.cloned.1.call-start = ((), (), s32[]{:S(2)}) async-start(), calls=%async_computation.12 | async-start | bytes 4259840
Sparse Core Ops, SparseCore 0:
  561.0 81.9 all-gather.2
  674.7 145.5 reduce-scatter.3
